TPU v7x, 512 devices: a whole 4x8x8 slice. The times are simulated.
512 devices in a mesh: aux: 8 (over z), ao: 16 (over y, core), orb: 4 (over x).
Axes of the slice: x: 4, y: 8, z: 8, core: 2. Of those that a mesh axis runs over, the one named last changes fastest.
Arguments:
- integrals: bfloat16 [128, 16, 4, 128, 128], P('aux', 'ao', None, 'orb'), may hold values from -6 to 6
- partner: int32 [16, 4], P('ao'), may hold values from 0 to 15
- pair_count: int32 [16], P('ao'), may hold values from 1 to 4
- occupied_coeff: bfloat16 [2048, 512], P('ao', 'orb'), may hold values from -0.25 to 0.25
- occupied_domain: int32 [16, 4], P('ao', 'orb'), may hold values 0 or 1
- virtual_coeff: bfloat16 [2048, 8192], P('aux', 'ao'), may hold values from -0.125 to 0.125
- virtual_domain: int32 [16, 64], P(None, 'ao'), may hold values 0 or 1
Outputs:
- transformed: bfloat16 [128, 512, 8192], P('aux', 'orb', 'ao')
All inputs are finite; a program needn't handle non-finite values. No bound on the sum of `occupied_domain` or of `virtual_domain` on one device may be relied on, other than what follows from the above.
Results may differ from a plain program's by a relative error of at most 0.0049.
Values may be sent and summed in bfloat16 or wider, within the bound.
A program may use at most 64 MiB of HBM per device.

v0:
```python
import jax
import jax.numpy as jnp
from jax import lax
from jax.sharding import PartitionSpec as P


def local(
    integrals, partner, pair_count, occupied_coeff, occupied_domain, virtual_coeff, virtual_domain
):
    block_size = integrals.shape[4]
    slab_rows = integrals.shape[0]
    local_blocks = integrals.shape[1]
    slot_count = integrals.shape[2]
    occ_width = occupied_coeff.shape[1]
    domain_wire = occupied_domain.astype(jnp.bfloat16)
    all_occ, all_domain = (
        lax.all_gather(occupied_coeff, "ao", axis=0, tiled=True),
        lax.all_gather(domain_wire, "ao", axis=0, tiled=True),
    )
    occ_mask = jnp.repeat(jnp.repeat(all_domain, block_size, axis=0), block_size, axis=1)
    occ_masked = all_occ * occ_mask
    block_total = all_domain.shape[0]
    picked = occ_masked.reshape(block_total, block_size, occ_width)[partner]
    slots = jnp.arange(slot_count, dtype=jnp.int32)
    live = (slots[None, :] < pair_count[:, None]).astype(jnp.bfloat16)
    picked = picked * live[:, :, None, None]
    all_columns = lax.all_to_all(picked, "orb", split_axis=2, concat_axis=3, tiled=True)
    partial_term = jnp.einsum(
        "nkri,pnkrv->pinv", all_columns, integrals, preferred_element_type=jnp.float32
    )
    half_wide = lax.psum_scatter(partial_term, "orb", scatter_dimension=1, tiled=True)
    half_local = half_wide.reshape(slab_rows, occ_width, local_blocks * block_size).astype(
        jnp.bfloat16
    )
    vir_rows = lax.all_gather(virtual_coeff, "aux", axis=0, tiled=True)
    vir_mask = jnp.repeat(
        jnp.repeat(virtual_domain, block_size, axis=0), block_size, axis=1
    ).astype(jnp.bfloat16)
    vir_masked = vir_rows * vir_mask
    vir_width = vir_masked.shape[1]
    piece = lax.all_gather(half_local, "ao", axis=2, tiled=True)
    count = piece.shape[2]
    flat = piece.reshape(slab_rows * occ_width, count)
    product = jnp.dot(flat, vir_masked, preferred_element_type=jnp.float32)
    result = product.reshape(slab_rows, occ_width, vir_width)
    return result.astype(jnp.bfloat16)


def solution(mesh):
    placed = (
        P("aux", "ao", None, "orb", None),
        P("ao", None),
        P("ao"),
        P("ao", "orb"),
        P("ao", "orb"),
        P("aux", "ao"),
        P(None, "ao"),
    )
    return jax.shard_map(
        local, mesh=mesh, in_specs=placed, out_specs=P("aux", "orb", "ao"), check_vma=False
    )
```

profile of v0, /device:TPU:1, one launch (start us, length us, event | category | flops | bytes accessed | tf_op | source)
XLA Modules:
  0.0 215.5 jit_solution(4892264346600140509)
XLA Ops:
  7.4 0.0 copy-start
  7.4 0.0 reduce-scatter.2.cloned.1.call-start
  8.7 0.7 fusion.11
  9.4 1.3 dynamic-slice
  10.7 0.7 dynamic-update-slice
  11.3 29.8 %all-reduce = bf16[16]{0:T(256)(128)(2,1)S(1)} all-reduce(bf16[16]{0:T(256)(128)(2,1)S(1)} %dynamic-update-slice), channel_id=1, replica_groups=mesh['aux'=8,'ao'=16,'orb'=4] {'ao'}, use_global_device_ids=true, to_apply=%add | all-reduce | flops 16 | bytes 64
  41.1 0.1 broadcast_bitcast_fusion
  41.2 16.4 %all_gather.14 = bf16[2048,128]{1,0:T(8,128)(2,1)S(1)} all-gather(bf16[128,128]{1,0:T(8,128)(2,1)} %param.10), channel_id=1, replica_groups=mesh['aux'=8,'ao'=16,'orb'=4] {'ao'}, dimensions={0}, use_global_device_ids=true | all-gather | bytes 557056 | tf_op jit(solution)/shard_map/all_gather | solution.py:17
  57.6 0.3 broadcast_multiply_fusion
  58.0 0.6 gather_fusion
  58.5 0.1 bitcast_multiply_fusion.1
  58.6 0.1 copy.14
  58.7 7.3 %all_to_all.15 = bf16[1,4,128,128]{3,1,0,2:T(4,128)(2,1)S(1)} all-to-all(bf16[1,4,128,128]{3,1,0,2:T(4,128)(2,1)S(1)} %copy.14), channel_id=1, replica_groups=mesh['aux'=8,'ao'=16,'orb'=4] {'orb'}, dimensions={2} | all-to-all | bytes 262144 | tf_op jit(solution)/shard_map/all_to_all | solution.py:27
  66.1 0.1 copy.16
  66.1 0.1 reshape.70
  66.2 0.0 copy-done
  66.2 2.7 %convolution_bitcast_fusion = f32[16,512,1,128]{3,1,0,2:T(8,128)} fusion(bf16[4,32,512,1]{2,1,0,3:T(8,128)(2,1)S(1)} %reshape.70, bf16[16,1,4,32,128]{4,3,2,1,0:T(8,128)(2,1)S(1)} %copy-done), kind=kOutput, calls=%fused_computation.3 | convolution fusion | flops 268435456 | bytes 4849664 | tf_op jit(solution)/shard_map/nkri,pnkrv->pinv/dot_general | solution.py:28
  68.9 0.0 reduce-scatter.2.cloned.1.call-update
  68.9 0.0 copy-start.1
  68.9 0.0 all-gather.4.cloned.1.call-start
  69.0 0.5 all-gather.4.cloned.1.call-update
  69.5 0.0 all-gather.6.cloned.1.call-start
  69.6 51.7 %reduce-scatter.2.cloned.1.call-done = f32[16,128,1,128]{3,1,0,2:T(8,128)} async-done(((f32[16,512,1,128]{3,1,0,2:T(8,128)}), f32[16,128,1,128]{3,1,0,2:T(8,128)}) %reduce-scatter.2.cloned.1.call-update) | async-done | bytes 1048592 | tf_op jit(solution)/shard_map/reduce_scatter | solution.py:31
  121.2 2.1 convert_element_type.34
  123.3 0.0 all-gather.6.cloned.1.call-update
  123.4 0.0 copy-done.1
  123.4 0.1 copy.17
  123.5 0.0 all-gather.4.cloned.1.call-done
  123.5 0.0 copy-start.2
  123.5 69.4 %all-gather.6.cloned.1.call-done = bf16[16,128,1,2048]{3,1,0,2:T(8,128)(2,1)} async-done(((bf16[16,128,1,128]{3,1,0,2:T(8,128)(2,1)}), bf16[16,128,1,2048]{3,1,0,2:T(8,128)(2,1)}) %all-gather.6.cloned.1.call-update) | async-done | bytes 8388624 | tf_op jit(solution)/shard_map/all_gather | solution.py:41
  192.9 0.1 broadcast_in_dim.21
  193.0 5.8 %broadcast_in_dim.22 = bf16[2048,4,128]{2,1,0:T(4,128)(2,1)S(1)} broadcast(bf16[2048,4]{1,0:T(8,128)(2,1)S(1)} %bitcast.47), dimensions={0,1} | broadcast | bytes 2113536 | tf_op jit(solution)/shard_map/broadcast_in_dim | solution.py:36
  198.7 0.0 copy-done.2
  198.8 9.3 %fusion.5 = bf16[16,128,512]{2,1,0:T(8,128)(2,1)} fusion(bf16[2048,512]{1,0:T(8,128)(2,1)S(1)} %copy-done.2, bf16[256,8,4,128]{3,2,1,0:T(4,128)(2,1)S(1)} %bitcast.46, bf16[16,128,1,2048]{3,1,0,2:T(8,128)(2,1)} %all-gather.6.cloned.1.call-done), kind=kOutput, calls=%fused_computation.7 | convolution fusion | flops 4297064448 | bytes 14680064 | tf_op jit(solution)/shard_map/dot_general | solution.py:44
  (5 shorter events, 0.0 us)
Async XLA Ops:
  7.4 58.8 %copy-start = (bf16[16,1,4,32,128]{4,3,2,1,0:T(8,128)(2,1)S(1)}, bf16[16,1,4,32,128]{4,3,2,1,0:T(8,128)(2,1)}, u32[]{:S(2)}) copy-start(bf16[16,1,4,32,128]{4,3,2,1,0:T(8,128)(2,1)} %param.7) | copy-start | bytes 1572868
  7.4 113.9 %reduce-scatter.2.cloned.1.call-start = ((), (), s32[]{:S(2)}) async-start(), calls=%async_computation.2 | async-start | bytes 5242880 | tf_op jit(solution)/shard_map/reduce_scatter | solution.py:31
  68.9 54.5 %copy-start.1 = (s32[16,4]{0,1:T(4,128)S(1)}, s32[16,4]{0,1:T(4,128)}, u32[]{:S(2)}) copy-start(s32[16,4]{0,1:T(4,128)} %param.13) | copy-start | bytes 772
  68.9 54.6 %all-gather.4.cloned.1.call-start = ((), (), s32[]{:S(2)}) async-start(), calls=%async_computation.3 | async-start | bytes 2359296 | tf_op jit(solution)/shard_map/all_gather | solution.py:35
  69.5 123.4 %all-gather.6.cloned.1.call-start = ((), (), s32[]{:S(2)}) async-start(), calls=%async_computation.4 | async-start | bytes 8912896 | tf_op jit(solution)/shard_map/all_gather | solution.py:41
  123.5 75.3 %copy-start.2 = (bf16[2048,512]{1,0:T(8,128)(2,1)S(1)}, bf16[2048,512]{1,0:T(8,128)(2,1)}, u32[]{:S(2)}) copy-start(bf16[2048,512]{1,0:T(8,128)(2,1)} %all-gather.4.cloned.1.call-done) | copy-start | bytes 6291460
Sparse Core Ops, SparseCore 0:
  69.0 52.1 reduce-scatter.1
Sparse Core Ops, SparseCore 1:
  71.5 40.2 all-gather.3
  123.5 69.4 all-gather.5
where the time goes:
time: 216 us
  waiting for transfers between devices  122 us (56%)
  blocking collectives  53.5 us (25%)
  between operations  16.3 us (8%)
  matrix products  12 us (6%)
  local copies, waits for them, and re-layouts  8.79 us (4%)
  other arithmetic  3.2 us (1%)
    all_gather x1, waiting for transfers between devices, local(): piece = lax.all_gather(half_local, 'ao', axis=2, tiled=True)  69.4 us
    reduce_scatter x1, waiting for transfers between devices, local(): lax.psum_scatter(partial_term, 'orb', scatter_dimension=1, tiled=True)  51.7 us
    unnamed x1, blocking collectives  29.8 us
    all_gather x1, blocking collectives, local(): lax.all_gather(occupied_coeff, 'ao', axis=0, tiled=True)  16.4 us
    dot_general x1, matrix products, local(): product = jnp.dot(flat, vir_masked, preferred_element_type=jnp.float32)  9.32 us
    all_to_all x1, blocking collectives, local(): lax.all_to_all(picked, 'orb', split_axis=2, concat_axis=3, tiled=True)  7.31 us
    broadcast_in_dim x1, local copies, waits for them, and re-layouts, local(): jnp.repeat(jnp.repeat(virtual_domain, block_size, axis=0), block_size, ax...  5.78 us
  transfers between devices with their start and end apart: 3, of which 2 were waited for; matrix products, arithmetic and copies ran while one was open for 1% of the time, Pallas kernels for 0%

commit v1 on v0

--- a/solution.py
+++ b/solution.py
@@ -24,7 +24,12 @@
     slots = jnp.arange(slot_count, dtype=jnp.int32)
     live = (slots[None, :] < pair_count[:, None]).astype(jnp.bfloat16)
     picked = picked * live[:, :, None, None]
-    all_columns = lax.all_to_all(picked, "orb", split_axis=2, concat_axis=3, tiled=True)
+    all_columns = jnp.concatenate(
+        lax.all_to_all(
+            jnp.stack(jnp.split(picked, lax.axis_size("orb"), axis=2), axis=0), "orb", 0, 0
+        ),
+        axis=3,
+    )
     partial_term = jnp.einsum(
         "nkri,pnkrv->pinv", all_columns, integrals, preferred_element_type=jnp.float32
     )

time: 216 us -> 216 us (level)
  no operation moved by 1% of the time
where the time goes in v1:
time: 216 us
  waiting for transfers between devices  122 us (56%)
  blocking collectives  53.5 us (25%)
  between operations  16.3 us (8%)
  matrix products  12 us (6%)
  local copies, waits for them, and re-layouts  8.91 us (4%)
  other arithmetic  3.22 us (1%)
    all_gather x1, waiting for transfers between devices, local(): piece = lax.all_gather(half_local, 'ao', axis=2, tiled=True)  69.4 us
    reduce_scatter x1, waiting for transfers between devices, local(): lax.psum_scatter(partial_term, 'orb', scatter_dimension=1, tiled=True)  51.7 us
    unnamed x1, blocking collectives  29.8 us
    all_gather x1, blocking collectives, local(): lax.all_gather(occupied_coeff, 'ao', axis=0, tiled=True)  16.4 us
    dot_general x1, matrix products, local(): product = jnp.dot(flat, vir_masked, preferred_element_type=jnp.float32)  9.32 us
    all_to_all x1, blocking collectives, local(): lax.all_to_all(jnp.stack(jnp.split(picked, lax.axis_size('orb'), axis=2),...  7.31 us
    broadcast_in_dim x1, local copies, waits for them, and re-layouts, local(): jnp.repeat(jnp.repeat(virtual_domain, block_size, axis=0), block_size, ax...  5.78 us
  transfers between devices with their start and end apart: 3, of which 2 were waited for; matrix products, arithmetic and copies ran while one was open for 1% of the time, Pallas kernels for 0%

profile of v1, /device:TPU:1, one launch (start us, length us, event | category | flops | bytes accessed | tf_op | source)
XLA Modules:
  0.0 215.6 jit_solution(4295837192295602892)
XLA Ops:
  7.4 0.0 copy-start
  7.4 0.0 reduce-scatter.2.cloned.1.call-start
  8.7 0.7 fusion.11
  9.4 1.3 dynamic-slice
  10.7 0.8 dynamic-update-slice
  11.5 29.8 %all-reduce = bf16[16]{0:T(256)(128)(2,1)S(1)} all-reduce(bf16[16]{0:T(256)(128)(2,1)S(1)} %dynamic-update-slice), channel_id=1, replica_groups=mesh['aux'=8,'ao'=16,'orb'=4] {'ao'}, use_global_device_ids=true, to_apply=%add | all-reduce | flops 16 | bytes 64
  41.3 0.1 broadcast_bitcast_fusion
  41.4 16.4 %all_gather.14 = bf16[2048,128]{1,0:T(8,128)(2,1)S(1)} all-gather(bf16[128,128]{1,0:T(8,128)(2,1)} %param.10), channel_id=1, replica_groups=mesh['aux'=8,'ao'=16,'orb'=4] {'ao'}, dimensions={0}, use_global_device_ids=true | all-gather | bytes 557056 | tf_op jit(solution)/shard_map/all_gather | solution.py:17
  57.8 0.3 broadcast_multiply_fusion
  58.2 0.6 gather_fusion
  58.7 0.1 bitcast_multiply_fusion.1
  58.9 7.3 %all_to_all.5 = bf16[4,1,4,32,128]{4,3,2,1,0:T(8,128)(2,1)S(1)} all-to-all(bf16[4,1,4,32,128]{4,3,2,1,0:T(8,128)(2,1)S(1)} %pad_maximum_fusion), channel_id=1, replica_groups=mesh['aux'=8,'ao'=16,'orb'=4] {'orb'}, dimensions={0} | all-to-all | bytes 262144 | tf_op jit(solution)/shard_map/all_to_all | solution.py:28
  66.2 0.1 copy.12
  66.3 0.1 reshape.75
  66.3 0.0 copy-done
  66.4 2.7 %convolution_bitcast_fusion = f32[16,512,1,128]{3,1,0,2:T(8,128)} fusion(bf16[4,32,512,1]{2,1,0,3:T(8,128)(2,1)S(1)} %reshape.75, bf16[16,1,4,32,128]{4,3,2,1,0:T(8,128)(2,1)S(1)} %copy-done), kind=kOutput, calls=%fused_computation.3 | convolution fusion | flops 268435456 | bytes 4849664 | tf_op jit(solution)/shard_map/nkri,pnkrv->pinv/dot_general | solution.py:33
  69.0 0.0 reduce-scatter.2.cloned.1.call-update
  69.1 0.0 copy-start.1
  69.1 0.0 all-gather.4.cloned.1.call-start
  69.1 0.5 all-gather.4.cloned.1.call-update
  69.7 0.0 all-gather.6.cloned.1.call-start
  69.7 51.7 %reduce-scatter.2.cloned.1.call-done = f32[16,128,1,128]{3,1,0,2:T(8,128)} async-done(((f32[16,512,1,128]{3,1,0,2:T(8,128)}), f32[16,128,1,128]{3,1,0,2:T(8,128)}) %reduce-scatter.2.cloned.1.call-update) | async-done | bytes 1048592 | tf_op jit(solution)/shard_map/reduce_scatter | solution.py:36
  121.4 2.1 convert_element_type.34
  123.5 0.0 all-gather.6.cloned.1.call-update
  123.5 0.0 copy-done.1
  123.5 0.1 copy.13
  123.6 0.0 all-gather.4.cloned.1.call-done
  123.6 0.0 copy-start.2
  123.6 69.4 %all-gather.6.cloned.1.call-done = bf16[16,128,1,2048]{3,1,0,2:T(8,128)(2,1)} async-done(((bf16[16,128,1,128]{3,1,0,2:T(8,128)(2,1)}), bf16[16,128,1,2048]{3,1,0,2:T(8,128)(2,1)}) %all-gather.6.cloned.1.call-update) | async-done | bytes 8388624 | tf_op jit(solution)/shard_map/all_gather | solution.py:46
  193.0 0.1 broadcast_in_dim.21
  193.1 5.8 %broadcast_in_dim.22 = bf16[2048,4,128]{2,1,0:T(4,128)(2,1)S(1)} broadcast(bf16[2048,4]{1,0:T(8,128)(2,1)S(1)} %bitcast.53), dimensions={0,1} | broadcast | bytes 2113536 | tf_op jit(solution)/shard_map/broadcast_in_dim | solution.py:41
  198.9 0.0 copy-done.2
  198.9 9.3 %fusion.5 = bf16[16,128,512]{2,1,0:T(8,128)(2,1)} fusion(bf16[2048,512]{1,0:T(8,128)(2,1)S(1)} %copy-done.2, bf16[256,8,4,128]{3,2,1,0:T(4,128)(2,1)S(1)} %bitcast.52, bf16[16,128,1,2048]{3,1,0,2:T(8,128)(2,1)} %all-gather.6.cloned.1.call-done), kind=kOutput, calls=%fused_computation.7 | convolution fusion | flops 4297064448 | bytes 14680064 | tf_op jit(solution)/shard_map/dot_general | solution.py:49
  (6 shorter events, 0.0 us)
Async XLA Ops:
  7.4 59.0 %copy-start = (bf16[16,1,4,32,128]{4,3,2,1,0:T(8,128)(2,1)S(1)}, bf16[16,1,4,32,128]{4,3,2,1,0:T(8,128)(2,1)}, u32[]{:S(2)}) copy-start(bf16[16,1,4,32,128]{4,3,2,1,0:T(8,128)(2,1)} %param.7) | copy-start | bytes 1572868
  7.4 114.0 %reduce-scatter.2.cloned.1.call-start = ((), (), s32[]{:S(2)}) async-start(), calls=%async_computation.2 | async-start | bytes 5242880 | tf_op jit(solution)/shard_map/reduce_scatter | solution.py:36
  69.1 54.5 %copy-start.1 = (s32[16,4]{0,1:T(4,128)S(1)}, s32[16,4]{0,1:T(4,128)}, u32[]{:S(2)}) copy-start(s32[16,4]{0,1:T(4,128)} %param.13) | copy-start | bytes 772
  69.1 54.6 %all-gather.4.cloned.1.call-start = ((), (), s32[]{:S(2)}) async-start(), calls=%async_computation.3 | async-start | bytes 2359296 | tf_op jit(solution)/shard_map/all_gather | solution.py:40
  69.7 123.4 %all-gather.6.cloned.1.call-start = ((), (), s32[]{:S(2)}) async-start(), calls=%async_computation.4 | async-start | bytes 8912896 | tf_op jit(solution)/shard_map/all_gather | solution.py:46
  123.6 75.3 %copy-start.2 = (bf16[2048,512]{1,0:T(8,128)(2,1)S(1)}, bf16[2048,512]{1,0:T(8,128)(2,1)}, u32[]{:S(2)}) copy-start(bf16[2048,512]{1,0:T(8,128)(2,1)} %all-gather.4.cloned.1.call-done) | copy-start | bytes 6291460
Sparse Core Ops, SparseCore 0:
  69.2 52.1 reduce-scatter.1
Sparse Core Ops, SparseCore 1:
  71.6 40.1 all-gather.3
  123.6 69.4 all-gather.5
